TPU v7x, 256 devices: a whole 4x4x8 slice. The times are simulated.
256 devices in a mesh: blk: 16 (over z, core), segment: 2 (over y_hi), rep: 8 (over x, y_lo).
Axes of the slice: x: 4, y: 4 (y_hi: 2, y_lo: 2; y = y_hi * 2 + y_lo), z: 8, core: 2. Of those that a mesh axis runs over, the one named last changes fastest.
Arguments:
- features: bfloat16 [16384, 256], P('blk'), may hold values from -14 to 14
- tile_weight: bfloat16 [49152, 128, 128], P(('blk', 'segment', 'rep')), may hold values from -0.099609375 to 0.099609375
- tile_limit: int32 [49152, 128], P(('blk', 'segment', 'rep')), may hold values from 1 to 128
- tile_src: int32 [49152, 1], P(('blk', 'segment', 'rep')), may hold values from 0 to 15; in each aligned block of 192 rows (0 to 191, 192 to 383, ...) at most 24 rows name the same one
- tile_row: int32 [49152], P(('blk', 'segment', 'rep')), may hold values from 0 to 5
- tile_col: int32 [49152], P(('blk', 'segment', 'rep')), may hold values from 0 to 7
- gain_one: float32 [256], replicated, may hold values from 0.25 to 1.75
- up_one: bfloat16 [256, 1024], replicated, may hold values from -0.375 to 0.375
- down_one: bfloat16 [1024, 256], replicated, may hold values from -0.25 to 0.25
- gain_two: float32 [256], replicated, may hold values from 0.25 to 1.75
- gate_two: bfloat16 [256, 2048], P(None, ('segment', 'rep')), may hold values from -0.375 to 0.375
- up_two: bfloat16 [256, 2048], P(None, ('segment', 'rep')), may hold values from -0.375 to 0.375
- down_two: bfloat16 [256, 2048], P(None, ('segment', 'rep')), may hold values from -0.25 to 0.25
Outputs:
- readout: bfloat16 [196608, 256], P(('blk', 'segment', 'rep'))
Inputs may be any that keep to these rules, and one draw needn't show every extreme that they name: `tile_src`: among the 192 tiles of one device at most 24 name the same partition, a bound that some block reaches.
All inputs are finite; a program needn't handle non-finite values.
Results may differ from a plain program's by a relative error of at most 0.0062.
Values may be sent and summed in bfloat16 or wider, within the bound.
No kernel may reach another device: no remote copies, remote signals or barrier semaphores. Data moves between devices by JAX's collectives and lax.ppermute only.
A program may use at most 128 MiB of HBM per device.

v0:
```python
import jax
import jax.numpy as jnp
from jax import lax
from jax.sharding import PartitionSpec as P

FEATURES = 256
TILE_SIZE = 128
SRC_BLOCK = 1024
DEST_DEV = 768
TILE_COUNT = 192
SLOT_CAP = 24


def rms_scaled(values, norm_gain):
    mean_square = jnp.mean(values * values, axis=-1, keepdims=True)
    return values * lax.rsqrt(mean_square + 1e-06) * norm_gain


def local(
    features,
    tile_weight,
    tile_limit,
    tile_src,
    tile_row,
    tile_col,
    gain_one,
    up_one,
    down_one,
    gain_two,
    gate_two,
    up_two,
    down_two,
):
    row_tiles = DEST_DEV // TILE_SIZE
    col_tiles = SRC_BLOCK // TILE_SIZE
    columns = jnp.arange(TILE_SIZE, dtype=jnp.int32)
    row_ids = jnp.arange(row_tiles, dtype=jnp.int32)
    masked = jnp.where(
        columns[None, None, :] < tile_limit[:, :, None],
        tile_weight,
        jnp.zeros((), tile_weight.dtype),
    )
    sources = tile_src[:, 0]
    partitions = lax.axis_size("blk")
    part_ids = jnp.arange(partitions, dtype=jnp.int32)
    member = (sources[:, None] == part_ids[None, :]).astype(jnp.int32)
    rank_table = jnp.cumsum(member, axis=0) - 1
    rank_held = jnp.sum(rank_table * member, axis=1)
    slot_ids = jnp.arange(SLOT_CAP, dtype=jnp.int32)
    slot_match = member[:, :, None] * (rank_held[:, None, None] == slot_ids[None, None, :]).astype(
        jnp.int32
    )
    tile_ids = jnp.arange(TILE_COUNT, dtype=jnp.int32)
    slot_tile = jnp.sum(slot_match * tile_ids[:, None, None], axis=0)
    slot_live = jnp.sum(slot_match, axis=0).astype(jnp.float32)
    zero_rows = jnp.zeros((row_tiles, TILE_SIZE, FEATURES), jnp.float32)
    source_piece = lax.all_gather(features, "blk", axis=0, tiled=True)
    block_count = source_piece.shape[0] // SRC_BLOCK

    def one_block(block_step, running):
        chosen = lax.dynamic_index_in_dim(slot_tile, block_step, 0, keepdims=False)
        live_now = lax.dynamic_index_in_dim(slot_live, block_step, 0, keepdims=False)
        source_tiles = lax.dynamic_slice_in_dim(source_piece, block_step * SRC_BLOCK, SRC_BLOCK, 0)
        source_tiles = source_tiles.reshape(col_tiles, TILE_SIZE, FEATURES)
        picked = source_tiles[tile_col[chosen]]
        contrib = jnp.einsum(
            "sij,sjf->sif", masked[chosen], picked, preferred_element_type=jnp.float32
        )
        onehot = (tile_row[chosen][:, None] == row_ids[None, :]).astype(jnp.float32) * live_now[
            :, None
        ]
        return running + jnp.einsum("sr,sif->rif", onehot, contrib, precision=lax.Precision.HIGHEST)

    summed = lax.fori_loop(0, block_count, one_block, zero_rows)
    aggregated = summed.reshape(DEST_DEV, FEATURES)
    normed_one = rms_scaled(aggregated, gain_one).astype(jnp.bfloat16)
    hidden_one = jnp.maximum(
        jnp.dot(normed_one, up_one, preferred_element_type=jnp.float32), 0.0
    ).astype(jnp.bfloat16)
    section_one = aggregated + jnp.dot(hidden_one, down_one, preferred_element_type=jnp.float32)
    normed_two = rms_scaled(section_one, gain_two).astype(jnp.bfloat16)
    gate_value = jnp.dot(
        normed_two,
        lax.all_gather(gate_two, ("segment", "rep"), axis=1, tiled=True),
        preferred_element_type=jnp.float32,
    )
    up_value = jnp.dot(
        normed_two,
        lax.all_gather(up_two, ("segment", "rep"), axis=1, tiled=True),
        preferred_element_type=jnp.float32,
    )
    hidden_two = (jax.nn.silu(gate_value) * up_value).astype(jnp.bfloat16)
    branch_two = lax.dot_general(
        hidden_two,
        lax.all_gather(down_two, ("segment", "rep"), axis=1, tiled=True),
        (((1,), (1,)), ((), ())),
        preferred_element_type=jnp.float32,
    )
    return (section_one + branch_two).astype(jnp.bfloat16)


def solution(mesh):
    in_specs = (
        P("blk", None),
        P(("blk", "segment", "rep"), None, None),
        P(("blk", "segment", "rep"), None),
        P(("blk", "segment", "rep"), None),
        P(("blk", "segment", "rep")),
        P(("blk", "segment", "rep")),
        P(),
        P(),
        P(),
        P(),
        P(None, ("segment", "rep")),
        P(None, ("segment", "rep")),
        P(None, ("segment", "rep")),
    )
    out_specs = P(("blk", "segment", "rep"), None)
    return jax.shard_map(local, mesh=mesh, in_specs=in_specs, out_specs=out_specs, check_vma=False)
```

profile of v0, /device:TPU:1, one launch (start us, length us, event | category | flops | bytes accessed | tf_op | source)
XLA Modules:
  0.0 340.6 jit_solution(471552748736940421)
XLA Ops:
  13.0 7.0 %fusion.17 = bf16[192,128,128]{2,1,0:T(8,128)(2,1)} fusion(bf16[192,128,128]{2,1,0:T(8,128)(2,1)} %param.16, s32[192,128]{1,0:T(8,128)} %param.17), kind=kLoop, calls=%fused_computation.27 | loop fusion | flops 6291456 | bytes 12681216 | tf_op jit(solution)/shard_map/jit(_where)/select_n | solution.py:38
  20.0 49.2 %all-gather.5.cloned.1.call-done = bf16[16384,256]{1,0:T(8,128)(2,1)} async-done(((bf16[1024,256]{1,0:T(8,128)(2,1)}), bf16[16384,256]{1,0:T(8,128)(2,1)}) %all-gather.5.cloned.1.call-update) | async-done | bytes 8388624 | tf_op jit(solution)/shard_map/all_gather | solution.py:57
  69.2 247.6 %while.14 = (s32[]{:T(128)}, f32[6,128,256]{2,0,1:T(8,128)}, s32[16,24]{1,0:T(8,128)S(1)}, s32[192]{0:T(256)S(1)}, f32[16,24]{1,0:T(8,128)S(1)}, /*index=5*/bf16...) while((s32[]{:T(128)}, f32[6,128,256]{2,0,1:T(8,128)}, ...), condition=%wide.region_6.7_spmd.clone, body=%wide.region_5.6_spmd.clone.sunk | while | flops 258345392 | bytes 16000889 | solution.py:74
  71.7 3.5 %gather_fusion = bf16[24,128,128]{2,1,0:T(8,128)(2,1)S(1)} fusion(bf16[192,128,128]{2,1,0:T(8,128)(2,1)} %get-tuple-element.287, s32[1024]{0:T(1024)S(1)} %pad_clamp_fusion.4), kind=kCustom, calls=%fused_computation.1.clone.clone.1 | custom fusion | bytes 1572960 | tf_op jit(solution)/shard_map/while/body/eval_jaxpr/gather | solution.py:67
  75.2 2.2 fusion.64
  78.1 6.3 %fusion.66 = f32[6,128,256]{2,0,1:T(8,128)} fusion(f32[24,128,256]{2,1,0:T(8,128)} %fusion.64, f32[6,128,256]{2,0,1:T(8,128)} %get-tuple-element.271, pred[]{:T(512)S(6)} %compare.4, f32[24]{0:T(128)S(1)} %fusion.65, s32[24]{0:T(128)S(1)} %gather_fusion.3), kind=kOutput, calls=%fused_computation.7.clone.1 | convolution fusion | flops 57016608 | bytes 4718785 | tf_op jit(solution)/shard_map/while/body/eval_jaxpr/sr,sif->rif/dot_general | solution.py:72
  86.9 3.5 %gather_fusion = bf16[24,128,128]{2,1,0:T(8,128)(2,1)S(1)} fusion(bf16[192,128,128]{2,1,0:T(8,128)(2,1)} %get-tuple-element.287, s32[1024]{0:T(1024)S(1)} %pad_clamp_fusion.4), kind=kCustom, calls=%fused_computation.1.clone.clone.1 | custom fusion | bytes 1572960 | tf_op jit(solution)/shard_map/while/body/eval_jaxpr/gather | solution.py:67
  90.4 2.2 fusion.64
  93.3 6.6 %fusion.66 = f32[6,128,256]{2,0,1:T(8,128)} fusion(f32[24,128,256]{2,1,0:T(8,128)} %fusion.64, f32[6,128,256]{2,0,1:T(8,128)} %get-tuple-element.271, pred[]{:T(512)S(6)} %compare.4, f32[24]{0:T(128)S(1)} %fusion.65, s32[24]{0:T(128)S(1)} %gather_fusion.3), kind=kOutput, calls=%fused_computation.7.clone.1 | convolution fusion | flops 57016608 | bytes 4718785 | tf_op jit(solution)/shard_map/while/body/eval_jaxpr/sr,sif->rif/dot_general | solution.py:72
  102.5 3.5 %gather_fusion = bf16[24,128,128]{2,1,0:T(8,128)(2,1)S(1)} fusion(bf16[192,128,128]{2,1,0:T(8,128)(2,1)} %get-tuple-element.287, s32[1024]{0:T(1024)S(1)} %pad_clamp_fusion.4), kind=kCustom, calls=%fused_computation.1.clone.clone.1 | custom fusion | bytes 1572960 | tf_op jit(solution)/shard_map/while/body/eval_jaxpr/gather | solution.py:67
  106.0 2.2 fusion.64
  108.9 6.6 %fusion.66 = f32[6,128,256]{2,0,1:T(8,128)} fusion(f32[24,128,256]{2,1,0:T(8,128)} %fusion.64, f32[6,128,256]{2,0,1:T(8,128)} %get-tuple-element.271, pred[]{:T(512)S(6)} %compare.4, f32[24]{0:T(128)S(1)} %fusion.65, s32[24]{0:T(128)S(1)} %gather_fusion.3), kind=kOutput, calls=%fused_computation.7.clone.1 | convolution fusion | flops 57016608 | bytes 4718785 | tf_op jit(solution)/shard_map/while/body/eval_jaxpr/sr,sif->rif/dot_general | solution.py:72
  118.0 3.5 %gather_fusion = bf16[24,128,128]{2,1,0:T(8,128)(2,1)S(1)} fusion(bf16[192,128,128]{2,1,0:T(8,128)(2,1)} %get-tuple-element.287, s32[1024]{0:T(1024)S(1)} %pad_clamp_fusion.4), kind=kCustom, calls=%fused_computation.1.clone.clone.1 | custom fusion | bytes 1572960 | tf_op jit(solution)/shard_map/while/body/eval_jaxpr/gather | solution.py:67
  121.5 2.2 fusion.64
  124.4 6.6 %fusion.66 = f32[6,128,256]{2,0,1:T(8,128)} fusion(f32[24,128,256]{2,1,0:T(8,128)} %fusion.64, f32[6,128,256]{2,0,1:T(8,128)} %get-tuple-element.271, pred[]{:T(512)S(6)} %compare.4, f32[24]{0:T(128)S(1)} %fusion.65, s32[24]{0:T(128)S(1)} %gather_fusion.3), kind=kOutput, calls=%fused_computation.7.clone.1 | convolution fusion | flops 57016608 | bytes 4718785 | tf_op jit(solution)/shard_map/while/body/eval_jaxpr/sr,sif->rif/dot_general | solution.py:72
  133.4 3.5 %gather_fusion = bf16[24,128,128]{2,1,0:T(8,128)(2,1)S(1)} fusion(bf16[192,128,128]{2,1,0:T(8,128)(2,1)} %get-tuple-element.287, s32[1024]{0:T(1024)S(1)} %pad_clamp_fusion.4), kind=kCustom, calls=%fused_computation.1.clone.clone.1 | custom fusion | bytes 1572960 | tf_op jit(solution)/shard_map/while/body/eval_jaxpr/gather | solution.py:67
  136.9 2.2 fusion.64
  139.8 6.6 %fusion.66 = f32[6,128,256]{2,0,1:T(8,128)} fusion(f32[24,128,256]{2,1,0:T(8,128)} %fusion.64, f32[6,128,256]{2,0,1:T(8,128)} %get-tuple-element.271, pred[]{:T(512)S(6)} %compare.4, f32[24]{0:T(128)S(1)} %fusion.65, s32[24]{0:T(128)S(1)} %gather_fusion.3), kind=kOutput, calls=%fused_computation.7.clone.1 | convolution fusion | flops 57016608 | bytes 4718785 | tf_op jit(solution)/shard_map/while/body/eval_jaxpr/sr,sif->rif/dot_general | solution.py:72
  148.9 3.5 %gather_fusion = bf16[24,128,128]{2,1,0:T(8,128)(2,1)S(1)} fusion(bf16[192,128,128]{2,1,0:T(8,128)(2,1)} %get-tuple-element.287, s32[1024]{0:T(1024)S(1)} %pad_clamp_fusion.4), kind=kCustom, calls=%fused_computation.1.clone.clone.1 | custom fusion | bytes 1572960 | tf_op jit(solution)/shard_map/while/body/eval_jaxpr/gather | solution.py:67
  152.4 2.2 fusion.64
  155.3 6.6 %fusion.66 = f32[6,128,256]{2,0,1:T(8,128)} fusion(f32[24,128,256]{2,1,0:T(8,128)} %fusion.64, f32[6,128,256]{2,0,1:T(8,128)} %get-tuple-element.271, pred[]{:T(512)S(6)} %compare.4, f32[24]{0:T(128)S(1)} %fusion.65, s32[24]{0:T(128)S(1)} %gather_fusion.3), kind=kOutput, calls=%fused_computation.7.clone.1 | convolution fusion | flops 57016608 | bytes 4718785 | tf_op jit(solution)/shard_map/while/body/eval_jaxpr/sr,sif->rif/dot_general | solution.py:72
  164.4 3.5 %gather_fusion = bf16[24,128,128]{2,1,0:T(8,128)(2,1)S(1)} fusion(bf16[192,128,128]{2,1,0:T(8,128)(2,1)} %get-tuple-element.287, s32[1024]{0:T(1024)S(1)} %pad_clamp_fusion.4), kind=kCustom, calls=%fused_computation.1.clone.clone.1 | custom fusion | bytes 1572960 | tf_op jit(solution)/shard_map/while/body/eval_jaxpr/gather | solution.py:67
  170.9 6.6 %fusion.66 = f32[6,128,256]{2,0,1:T(8,128)} fusion(f32[24,128,256]{2,1,0:T(8,128)} %fusion.64, f32[6,128,256]{2,0,1:T(8,128)} %get-tuple-element.271, pred[]{:T(512)S(6)} %compare.4, f32[24]{0:T(128)S(1)} %fusion.65, s32[24]{0:T(128)S(1)} %gather_fusion.3), kind=kOutput, calls=%fused_computation.7.clone.1 | convolution fusion | flops 57016608 | bytes 4718785 | tf_op jit(solution)/shard_map/while/body/eval_jaxpr/sr,sif->rif/dot_general | solution.py:72
  179.9 3.5 %gather_fusion = bf16[24,128,128]{2,1,0:T(8,128)(2,1)S(1)} fusion(bf16[192,128,128]{2,1,0:T(8,128)(2,1)} %get-tuple-element.287, s32[1024]{0:T(1024)S(1)} %pad_clamp_fusion.4), kind=kCustom, calls=%fused_computation.1.clone.clone.1 | custom fusion | bytes 1572960 | tf_op jit(solution)/shard_map/while/body/eval_jaxpr/gather | solution.py:67
  183.4 2.2 fusion.64
  186.3 6.6 %fusion.66 = f32[6,128,256]{2,0,1:T(8,128)} fusion(f32[24,128,256]{2,1,0:T(8,128)} %fusion.64, f32[6,128,256]{2,0,1:T(8,128)} %get-tuple-element.271, pred[]{:T(512)S(6)} %compare.4, f32[24]{0:T(128)S(1)} %fusion.65, s32[24]{0:T(128)S(1)} %gather_fusion.3), kind=kOutput, calls=%fused_computation.7.clone.1 | convolution fusion | flops 57016608 | bytes 4718785 | tf_op jit(solution)/shard_map/while/body/eval_jaxpr/sr,sif->rif/dot_general | solution.py:72
  195.5 3.5 %gather_fusion = bf16[24,128,128]{2,1,0:T(8,128)(2,1)S(1)} fusion(bf16[192,128,128]{2,1,0:T(8,128)(2,1)} %get-tuple-element.287, s32[1024]{0:T(1024)S(1)} %pad_clamp_fusion.4), kind=kCustom, calls=%fused_computation.1.clone.clone.1 | custom fusion | bytes 1572960 | tf_op jit(solution)/shard_map/while/body/eval_jaxpr/gather | solution.py:67
  199.0 2.2 fusion.64
  201.9 6.6 %fusion.66 = f32[6,128,256]{2,0,1:T(8,128)} fusion(f32[24,128,256]{2,1,0:T(8,128)} %fusion.64, f32[6,128,256]{2,0,1:T(8,128)} %get-tuple-element.271, pred[]{:T(512)S(6)} %compare.4, f32[24]{0:T(128)S(1)} %fusion.65, s32[24]{0:T(128)S(1)} %gather_fusion.3), kind=kOutput, calls=%fused_computation.7.clone.1 | convolution fusion | flops 57016608 | bytes 4718785 | tf_op jit(solution)/shard_map/while/body/eval_jaxpr/sr,sif->rif/dot_general | solution.py:72
  210.9 3.5 %gather_fusion = bf16[24,128,128]{2,1,0:T(8,128)(2,1)S(1)} fusion(bf16[192,128,128]{2,1,0:T(8,128)(2,1)} %get-tuple-element.287, s32[1024]{0:T(1024)S(1)} %pad_clamp_fusion.4), kind=kCustom, calls=%fused_computation.1.clone.clone.1 | custom fusion | bytes 1572960 | tf_op jit(solution)/shard_map/while/body/eval_jaxpr/gather | solution.py:67
  214.4 2.2 fusion.64
  217.3 6.6 %fusion.66 = f32[6,128,256]{2,0,1:T(8,128)} fusion(f32[24,128,256]{2,1,0:T(8,128)} %fusion.64, f32[6,128,256]{2,0,1:T(8,128)} %get-tuple-element.271, pred[]{:T(512)S(6)} %compare.4, f32[24]{0:T(128)S(1)} %fusion.65, s32[24]{0:T(128)S(1)} %gather_fusion.3), kind=kOutput, calls=%fused_computation.7.clone.1 | convolution fusion | flops 57016608 | bytes 4718785 | tf_op jit(solution)/shard_map/while/body/eval_jaxpr/sr,sif->rif/dot_general | solution.py:72
  226.4 3.5 %gather_fusion = bf16[24,128,128]{2,1,0:T(8,128)(2,1)S(1)} fusion(bf16[192,128,128]{2,1,0:T(8,128)(2,1)} %get-tuple-element.287, s32[1024]{0:T(1024)S(1)} %pad_clamp_fusion.4), kind=kCustom, calls=%fused_computation.1.clone.clone.1 | custom fusion | bytes 1572960 | tf_op jit(solution)/shard_map/while/body/eval_jaxpr/gather | solution.py:67
  232.8 6.6 %fusion.66 = f32[6,128,256]{2,0,1:T(8,128)} fusion(f32[24,128,256]{2,1,0:T(8,128)} %fusion.64, f32[6,128,256]{2,0,1:T(8,128)} %get-tuple-element.271, pred[]{:T(512)S(6)} %compare.4, f32[24]{0:T(128)S(1)} %fusion.65, s32[24]{0:T(128)S(1)} %gather_fusion.3), kind=kOutput, calls=%fused_computation.7.clone.1 | convolution fusion | flops 57016608 | bytes 4718785 | tf_op jit(solution)/shard_map/while/body/eval_jaxpr/sr,sif->rif/dot_general | solution.py:72
  241.9 3.5 %gather_fusion = bf16[24,128,128]{2,1,0:T(8,128)(2,1)S(1)} fusion(bf16[192,128,128]{2,1,0:T(8,128)(2,1)} %get-tuple-element.287, s32[1024]{0:T(1024)S(1)} %pad_clamp_fusion.4), kind=kCustom, calls=%fused_computation.1.clone.clone.1 | custom fusion | bytes 1572960 | tf_op jit(solution)/shard_map/while/body/eval_jaxpr/gather | solution.py:67
  248.3 6.6 %fusion.66 = f32[6,128,256]{2,0,1:T(8,128)} fusion(f32[24,128,256]{2,1,0:T(8,128)} %fusion.64, f32[6,128,256]{2,0,1:T(8,128)} %get-tuple-element.271, pred[]{:T(512)S(6)} %compare.4, f32[24]{0:T(128)S(1)} %fusion.65, s32[24]{0:T(128)S(1)} %gather_fusion.3), kind=kOutput, calls=%fused_computation.7.clone.1 | convolution fusion | flops 57016608 | bytes 4718785 | tf_op jit(solution)/shard_map/while/body/eval_jaxpr/sr,sif->rif/dot_general | solution.py:72
  257.4 3.5 %gather_fusion = bf16[24,128,128]{2,1,0:T(8,128)(2,1)S(1)} fusion(bf16[192,128,128]{2,1,0:T(8,128)(2,1)} %get-tuple-element.287, s32[1024]{0:T(1024)S(1)} %pad_clamp_fusion.4), kind=kCustom, calls=%fused_computation.1.clone.clone.1 | custom fusion | bytes 1572960 | tf_op jit(solution)/shard_map/while/body/eval_jaxpr/gather | solution.py:67
  260.9 2.2 fusion.64
  263.8 6.6 %fusion.66 = f32[6,128,256]{2,0,1:T(8,128)} fusion(f32[24,128,256]{2,1,0:T(8,128)} %fusion.64, f32[6,128,256]{2,0,1:T(8,128)} %get-tuple-element.271, pred[]{:T(512)S(6)} %compare.4, f32[24]{0:T(128)S(1)} %fusion.65, s32[24]{0:T(128)S(1)} %gather_fusion.3), kind=kOutput, calls=%fused_computation.7.clone.1 | convolution fusion | flops 57016608 | bytes 4718785 | tf_op jit(solution)/shard_map/while/body/eval_jaxpr/sr,sif->rif/dot_general | solution.py:72
  272.9 3.5 %gather_fusion = bf16[24,128,128]{2,1,0:T(8,128)(2,1)S(1)} fusion(bf16[192,128,128]{2,1,0:T(8,128)(2,1)} %get-tuple-element.287, s32[1024]{0:T(1024)S(1)} %pad_clamp_fusion.4), kind=kCustom, calls=%fused_computation.1.clone.clone.1 | custom fusion | bytes 1572960 | tf_op jit(solution)/shard_map/while/body/eval_jaxpr/gather | solution.py:67
  276.4 2.2 fusion.64
  279.3 6.6 %fusion.66 = f32[6,128,256]{2,0,1:T(8,128)} fusion(f32[24,128,256]{2,1,0:T(8,128)} %fusion.64, f32[6,128,256]{2,0,1:T(8,128)} %get-tuple-element.271, pred[]{:T(512)S(6)} %compare.4, f32[24]{0:T(128)S(1)} %fusion.65, s32[24]{0:T(128)S(1)} %gather_fusion.3), kind=kOutput, calls=%fused_computation.7.clone.1 | convolution fusion | flops 57016608 | bytes 4718785 | tf_op jit(solution)/shard_map/while/body/eval_jaxpr/sr,sif->rif/dot_general | solution.py:72
  288.4 3.5 %gather_fusion = bf16[24,128,128]{2,1,0:T(8,128)(2,1)S(1)} fusion(bf16[192,128,128]{2,1,0:T(8,128)(2,1)} %get-tuple-element.287, s32[1024]{0:T(1024)S(1)} %pad_clamp_fusion.4), kind=kCustom, calls=%fused_computation.1.clone.clone.1 | custom fusion | bytes 1572960 | tf_op jit(solution)/shard_map/while/body/eval_jaxpr/gather | solution.py:67
  294.8 6.6 %fusion.66 = f32[6,128,256]{2,0,1:T(8,128)} fusion(f32[24,128,256]{2,1,0:T(8,128)} %fusion.64, f32[6,128,256]{2,0,1:T(8,128)} %get-tuple-element.271, pred[]{:T(512)S(6)} %compare.4, f32[24]{0:T(128)S(1)} %fusion.65, s32[24]{0:T(128)S(1)} %gather_fusion.3), kind=kOutput, calls=%fused_computation.7.clone.1 | convolution fusion | flops 57016608 | bytes 4718785 | tf_op jit(solution)/shard_map/while/body/eval_jaxpr/sr,sif->rif/dot_general | solution.py:72
  303.9 3.5 %gather_fusion = bf16[24,128,128]{2,1,0:T(8,128)(2,1)S(1)} fusion(bf16[192,128,128]{2,1,0:T(8,128)(2,1)} %get-tuple-element.287, s32[1024]{0:T(1024)S(1)} %pad_clamp_fusion.4), kind=kCustom, calls=%fused_computation.1.clone.clone.1 | custom fusion | bytes 1572960 | tf_op jit(solution)/shard_map/while/body/eval_jaxpr/gather | solution.py:67
  310.3 6.6 %fusion.66 = f32[6,128,256]{2,0,1:T(8,128)} fusion(f32[24,128,256]{2,1,0:T(8,128)} %fusion.64, f32[6,128,256]{2,0,1:T(8,128)} %get-tuple-element.271, pred[]{:T(512)S(6)} %compare.4, f32[24]{0:T(128)S(1)} %fusion.65, s32[24]{0:T(128)S(1)} %gather_fusion.3), kind=kOutput, calls=%fused_computation.7.clone.1 | convolution fusion | flops 57016608 | bytes 4718785 | tf_op jit(solution)/shard_map/while/body/eval_jaxpr/sr,sif->rif/dot_general | solution.py:72
  322.3 5.0 %fusion.23 = f32[768,2048]{1,0:T(8,128)} fusion(bf16[256,2048]{1,0:T(8,128)(2,1)} %all-gather.7.cloned.1.call-done, f32[768,256]{0,1:T(8,128)S(1)} %get-tuple-element.208, f32[256]{0:T(256)S(1)} %copy-done.3, f32[768]{0:T(1024)S(1)} %add_rsqrt_fusion), kind=kOutput, calls=%fused_computation.41 | convolution fusion | flops 805896192 | bytes 8130560 | tf_op jit(solution)/shard_map/dot_general | solution.py:82
  327.3 5.8 %fusion.22 = bf16[768,256]{0,1:T(8,128)(2,1)S(1)} fusion(f32[768,256]{0,1:T(8,128)S(1)} %get-tuple-element.208, bf16[256,2048]{1,0:T(8,128)(2,1)} %all-gather.11.cloned.1.call-done, f32[768,2048]{1,0:T(8,128)} %fusion.23, bf16[256,2048]{1,0:T(8,128)(2,1)} %all-gather.9.cloned.1.call-done, f32[256]{0:T(256)S(1)} %copy-done.3, f32[768]{0:T(1024)S(1)} %add_rsqrt_fusion), kind=kOutput, calls=%fused_computation.34 | convolution fusion | flops 1621032960 | bytes 9572352 | tf_op jit(solution)/shard_map/dot_general | solution.py:93
  (191 shorter events, 74.5 us)
Async XLA Ops:
  6.5 313.6 %copy-start = (bf16[1024,256]{1,0:T(8,128)(2,1)S(1)}, bf16[1024,256]{1,0:T(8,128)(2,1)}, u32[]{:S(2)}) copy-start(bf16[1024,256]{1,0:T(8,128)(2,1)} %param.23) | copy-start | bytes 1572868
  6.5 62.7 %all-gather.5.cloned.1.call-start = ((), (), s32[]{:S(2)}) async-start(), calls=%async_computation | async-start | bytes 8912896 | tf_op jit(solution)/shard_map/all_gather | solution.py:57
  7.3 315.0 %all-gather.7.cloned.1.call-start = ((), (), s32[]{:S(2)}) async-start(), calls=%async_computation.1 | async-start | bytes 1114112 | tf_op jit(solution)/shard_map/all_gather | solution.py:84
  8.0 319.3 %all-gather.11.cloned.1.call-start = ((), (), s32[]{:S(2)}) async-start(), calls=%async_computation.3 | async-start | bytes 1114112 | tf_op jit(solution)/shard_map/all_gather | solution.py:95
  8.7 318.6 %all-gather.9.cloned.1.call-start = ((), (), s32[]{:S(2)}) async-start(), calls=%async_computation.2 | async-start | bytes 1114112 | tf_op jit(solution)/shard_map/all_gather | solution.py:89
  13.0 56.3 %copy-start.1 = (s32[192]{0:T(256)S(1)}, s32[192]{0:T(256)}, u32[]{:S(2)}) copy-start(s32[192]{0:T(256)} %param.19) | copy-start | bytes 2308
  13.0 56.3 %copy-start.2 = (s32[192]{0:T(256)S(1)}, s32[192]{0:T(256)}, u32[]{:S(2)}) copy-start(s32[192]{0:T(256)} %param.20) | copy-start | bytes 2308
  69.2 250.9 %copy-start.4 = (f32[256]{0:T(256)S(1)}, f32[256]{0:T(256)}, u32[]{:S(2)}) copy-start(f32[256]{0:T(256)} %param.21) | copy-start | bytes 3076
  316.9 5.4 %copy-start.3 = (f32[256]{0:T(256)S(1)}, f32[256]{0:T(256)}, u32[]{:S(2)}) copy-start(f32[256]{0:T(256)} %param.24) | copy-start | bytes 3076
Sparse Core Ops, SparseCore 0:
  9.2 60.0 all-gather.4
  70.9 55.6 all-gather.6
  128.3 68.4 all-gather.10
  198.4 68.3 all-gather.8
where the time goes:
time: 342 us; the launch traced here: 341 us
  matrix products  153 us (45%)
  local copies, waits for them, and re-layouts  109 us (32%)
  waiting for transfers between devices  51.9 us (15%)
  between operations  13.2 us (4%)
  other arithmetic  12.4 us (4%)
    dot_general x16, matrix products, one_block(): jnp.einsum('sr,sif->rif', onehot, contrib, precision=lax.Precision.HIGHEST)  105 us
    gather x16, local copies, waits for them, and re-layouts, one_block(): masked[chosen]  55.8 us
    all_gather x1, waiting for transfers between devices, local(): source_piece = lax.all_gather(features, 'blk', axis=0, tiled=True)  49.2 us
    dot_general x16, matrix products, one_block(): jnp.einsum('sij,sjf->sif', masked[chosen], picked, preferred_element_type...  34.9 us
    gather x32, local copies, waits for them, and re-layouts, one_block(): picked = source_tiles[tile_col[chosen]]  21.7 us
    dynamic_slice x16, local copies, waits for them, and re-layouts, one_block(): lax.dynamic_slice_in_dim(source_piece, block_step * SRC_BLOCK, SRC_BLOCK, 0)  17.2 us
    gather x16, local copies, waits for them, and re-layouts, one_block(): tile_row[chosen][:, None] == row_ids[None, :]  11.3 us
    select_n x1, other arithmetic, local(): jnp.where(columns[None, None, :] < tile_limit[:, :, None], tile_weight, j...  7.02 us
  transfers between devices with their start and end apart: 4, of which 1 were waited for; matrix products, arithmetic and copies ran while one was open for 79% of the time, Pallas kernels for 0%

commit v1 on v0

--- a/solution.py
+++ b/solution.py
@@ -54,7 +54,9 @@
     slot_tile = jnp.sum(slot_match * tile_ids[:, None, None], axis=0)
     slot_live = jnp.sum(slot_match, axis=0).astype(jnp.float32)
     zero_rows = jnp.zeros((row_tiles, TILE_SIZE, FEATURES), jnp.float32)
-    source_piece = lax.all_gather(features, "blk", axis=0, tiled=True)
+    source_piece = jnp.concatenate(
+        lax.all_to_all(jnp.stack([features] * lax.axis_size("blk")), "blk", 0, 0), axis=0
+    )
     block_count = source_piece.shape[0] // SRC_BLOCK
 
     def one_block(block_step, running):

time: 342 us -> 480 us (1.40)
  waiting for transfers between devices: 51.9 us -> 175 us
  starting transfers between devices: 0.12 us -> 10.2 us
  local copies, waits for them, and re-layouts: 109 us -> 114 us
    all_to_all x0 -> x1, waiting for transfers between devices: none -> 173 us  [local(): lax.all_to_all(jnp.stack([features] * lax.axis_size('blk')), 'blk', 0, 0)]
    all_gather x1 -> x0, waiting for transfers between devices: 49.2 us -> none  [local(): source_piece = lax.all_gather(features, 'blk', axis=0, tiled=True)]
    all_to_all x0 -> x1, starting transfers between devices: none -> 10.1 us  [local(): lax.all_to_all(jnp.stack([features] * lax.axis_size('blk')), 'blk', 0, 0)]
    another operation x1 -> x2, local copies, waits for them, and re-layouts: 0.01 us -> 5.12 us  [the longest x1 5.12 us: local(): jnp.stack([features] * lax.axis_size('blk'))]
  transfers between devices with their start and end apart: 4 -> 4, of which waited for: 1 -> 1; matrix products, arithmetic and copies ran while one was open for 79% -> 56% of each run, Pallas kernels for 0% -> 0%
where the time goes in v1:
time: 480 us; the launch traced here: 479 us
  waiting for transfers between devices  175 us (36%)
  matrix products  155 us (32%)
  local copies, waits for them, and re-layouts  114 us (24%)
  between operations  13.3 us (3%)
  starting transfers between devices  10.2 us (2%)
  other arithmetic  10 us (2%)
    all_to_all x1, waiting for transfers between devices, local(): lax.all_to_all(jnp.stack([features] * lax.axis_size('blk')), 'blk', 0, 0)  173 us
    dot_general x16, matrix products, one_block(): jnp.einsum('sr,sif->rif', onehot, contrib, precision=lax.Precision.HIGHEST)  105 us
    gather x16, local copies, waits for them, and re-layouts, one_block(): masked[chosen]  55.7 us
    dot_general x16, matrix products, one_block(): jnp.einsum('sij,sjf->sif', masked[chosen], picked, preferred_element_type...  37.1 us
    gather x32, local copies, waits for them, and re-layouts, one_block(): picked = source_tiles[tile_col[chosen]]  21.7 us
    dynamic_slice x16, local copies, waits for them, and re-layouts, one_block(): lax.dynamic_slice_in_dim(source_piece, block_step * SRC_BLOCK, SRC_BLOCK, 0)  17.2 us
    gather x16, local copies, waits for them, and re-layouts, one_block(): tile_row[chosen][:, None] == row_ids[None, :]  11.3 us
    all_to_all x1, starting transfers between devices, local(): lax.all_to_all(jnp.stack([features] * lax.axis_size('blk')), 'blk', 0, 0)  10.1 us
  transfers between devices with their start and end apart: 4, of which 1 were waited for; matrix products, arithmetic and copies ran while one was open for 56% of the time, Pallas kernels for 0%

profile of v1, /device:TPU:1, one launch (start us, length us, event | category | flops | bytes accessed | tf_op | source)
XLA Modules:
  0.0 478.6 jit_solution(1566297172717445849)
XLA Ops:
  6.5 5.1 %stack.2 = bf16[16,1024,256]{2,1,0:T(8,128)(2,1)} broadcast(bf16[1024,256]{1,0:T(8,128)(2,1)} %param.15), dimensions={1,2} | broadcast | bytes 8912896 | tf_op jit(solution)/shard_map/stack | solution.py:58
  11.7 10.1 %all-to-all-start = ((bf16[16,1024,256]{2,1,0:T(8,128)(2,1)}), bf16[16,1024,256]{2,1,0:T(8,128)(2,1)}, u32[]{:S(2)}, u32[]{:S(2)}) async-start(bf16[16,1024,256]{2,1,0:T(8,128)(2,1)} %stack.2), calls=%async_computation | async-start | bytes 16777216 | tf_op jit(solution)/shard_map/all_to_all | solution.py:58
  25.6 6.7 %fusion.17 = bf16[192,128,128]{2,1,0:T(8,128)(2,1)} fusion(bf16[192,128,128]{2,1,0:T(8,128)(2,1)} %param.16, s32[192,128]{1,0:T(8,128)S(1)} %copy-done.3), kind=kLoop, calls=%fused_computation.27 | loop fusion | flops 6291456 | bytes 12681216 | tf_op jit(solution)/shard_map/jit(_where)/select_n | solution.py:38
  32.3 172.8 %all-to-all-done = bf16[16,1024,256]{2,1,0:T(8,128)(2,1)} async-done(((bf16[16,1024,256]{2,1,0:T(8,128)(2,1)}), bf16[16,1024,256]{2,1,0:T(8,128)(2,1)}, u32[]{:S(2)}, u32[]{:S(2)}) %all-to-all-start) | async-done | bytes 8388640 | tf_op jit(solution)/shard_map/all_to_all | solution.py:58
  205.2 249.7 %while.14 = (s32[]{:T(128)}, f32[6,128,256]{2,0,1:T(8,128)}, s32[16,24]{1,0:T(8,128)S(1)}, s32[192]{0:T(256)S(1)}, f32[16,24]{1,0:T(8,128)S(1)}, /*index=5*/bf16...) while((s32[]{:T(128)}, f32[6,128,256]{2,0,1:T(8,128)}, ...), condition=%wide.region_6.7_spmd.clone, body=%wide.region_5.6_spmd.clone.sunk | while | flops 258345392 | bytes 16000889 | solution.py:76
  207.7 3.5 gather_fusion
  211.2 2.3 fusion.64
  214.2 6.3 %fusion.66 = f32[6,128,256]{2,0,1:T(8,128)} fusion(f32[24,128,256]{2,1,0:T(8,128)} %fusion.64, f32[6,128,256]{2,0,1:T(8,128)} %get-tuple-element.271, pred[]{:T(512)S(6)} %compare.4, f32[24]{0:T(128)S(1)} %fusion.65, s32[24]{0:T(128)S(1)} %gather_fusion.3), kind=kOutput, calls=%fused_computation.7.clone.1 | convolution fusion | flops 57016608 | bytes 4718785 | tf_op jit(solution)/shard_map/while/body/eval_jaxpr/sr,sif->rif/dot_general | solution.py:74
  223.0 3.5 gather_fusion
  226.5 2.3 fusion.64
  229.5 6.6 %fusion.66 = f32[6,128,256]{2,0,1:T(8,128)} fusion(f32[24,128,256]{2,1,0:T(8,128)} %fusion.64, f32[6,128,256]{2,0,1:T(8,128)} %get-tuple-element.271, pred[]{:T(512)S(6)} %compare.4, f32[24]{0:T(128)S(1)} %fusion.65, s32[24]{0:T(128)S(1)} %gather_fusion.3), kind=kOutput, calls=%fused_computation.7.clone.1 | convolution fusion | flops 57016608 | bytes 4718785 | tf_op jit(solution)/shard_map/while/body/eval_jaxpr/sr,sif->rif/dot_general | solution.py:74
  238.6 3.5 gather_fusion
  242.1 2.3 fusion.64
  245.2 6.6 %fusion.66 = f32[6,128,256]{2,0,1:T(8,128)} fusion(f32[24,128,256]{2,1,0:T(8,128)} %fusion.64, f32[6,128,256]{2,0,1:T(8,128)} %get-tuple-element.271, pred[]{:T(512)S(6)} %compare.4, f32[24]{0:T(128)S(1)} %fusion.65, s32[24]{0:T(128)S(1)} %gather_fusion.3), kind=kOutput, calls=%fused_computation.7.clone.1 | convolution fusion | flops 57016608 | bytes 4718785 | tf_op jit(solution)/shard_map/while/body/eval_jaxpr/sr,sif->rif/dot_general | solution.py:74
  254.2 3.5 gather_fusion
  257.7 2.3 fusion.64
  260.8 6.6 %fusion.66 = f32[6,128,256]{2,0,1:T(8,128)} fusion(f32[24,128,256]{2,1,0:T(8,128)} %fusion.64, f32[6,128,256]{2,0,1:T(8,128)} %get-tuple-element.271, pred[]{:T(512)S(6)} %compare.4, f32[24]{0:T(128)S(1)} %fusion.65, s32[24]{0:T(128)S(1)} %gather_fusion.3), kind=kOutput, calls=%fused_computation.7.clone.1 | convolution fusion | flops 57016608 | bytes 4718785 | tf_op jit(solution)/shard_map/while/body/eval_jaxpr/sr,sif->rif/dot_general | solution.py:74
  269.9 3.5 gather_fusion
  273.4 2.3 fusion.64
  276.4 6.6 %fusion.66 = f32[6,128,256]{2,0,1:T(8,128)} fusion(f32[24,128,256]{2,1,0:T(8,128)} %fusion.64, f32[6,128,256]{2,0,1:T(8,128)} %get-tuple-element.271, pred[]{:T(512)S(6)} %compare.4, f32[24]{0:T(128)S(1)} %fusion.65, s32[24]{0:T(128)S(1)} %gather_fusion.3), kind=kOutput, calls=%fused_computation.7.clone.1 | convolution fusion | flops 57016608 | bytes 4718785 | tf_op jit(solution)/shard_map/while/body/eval_jaxpr/sr,sif->rif/dot_general | solution.py:74
  285.5 3.5 gather_fusion
  289.0 2.3 fusion.64
  292.0 6.6 %fusion.66 = f32[6,128,256]{2,0,1:T(8,128)} fusion(f32[24,128,256]{2,1,0:T(8,128)} %fusion.64, f32[6,128,256]{2,0,1:T(8,128)} %get-tuple-element.271, pred[]{:T(512)S(6)} %compare.4, f32[24]{0:T(128)S(1)} %fusion.65, s32[24]{0:T(128)S(1)} %gather_fusion.3), kind=kOutput, calls=%fused_computation.7.clone.1 | convolution fusion | flops 57016608 | bytes 4718785 | tf_op jit(solution)/shard_map/while/body/eval_jaxpr/sr,sif->rif/dot_general | solution.py:74
  301.1 3.5 gather_fusion
  304.6 2.3 fusion.64
  307.6 6.6 %fusion.66 = f32[6,128,256]{2,0,1:T(8,128)} fusion(f32[24,128,256]{2,1,0:T(8,128)} %fusion.64, f32[6,128,256]{2,0,1:T(8,128)} %get-tuple-element.271, pred[]{:T(512)S(6)} %compare.4, f32[24]{0:T(128)S(1)} %fusion.65, s32[24]{0:T(128)S(1)} %gather_fusion.3), kind=kOutput, calls=%fused_computation.7.clone.1 | convolution fusion | flops 57016608 | bytes 4718785 | tf_op jit(solution)/shard_map/while/body/eval_jaxpr/sr,sif->rif/dot_general | solution.py:74
  316.7 3.5 gather_fusion
  320.2 2.3 fusion.64
  323.3 6.6 %fusion.66 = f32[6,128,256]{2,0,1:T(8,128)} fusion(f32[24,128,256]{2,1,0:T(8,128)} %fusion.64, f32[6,128,256]{2,0,1:T(8,128)} %get-tuple-element.271, pred[]{:T(512)S(6)} %compare.4, f32[24]{0:T(128)S(1)} %fusion.65, s32[24]{0:T(128)S(1)} %gather_fusion.3), kind=kOutput, calls=%fused_computation.7.clone.1 | convolution fusion | flops 57016608 | bytes 4718785 | tf_op jit(solution)/shard_map/while/body/eval_jaxpr/sr,sif->rif/dot_general | solution.py:74
  332.4 3.5 gather_fusion
  338.9 6.6 %fusion.66 = f32[6,128,256]{2,0,1:T(8,128)} fusion(f32[24,128,256]{2,1,0:T(8,128)} %fusion.64, f32[6,128,256]{2,0,1:T(8,128)} %get-tuple-element.271, pred[]{:T(512)S(6)} %compare.4, f32[24]{0:T(128)S(1)} %fusion.65, s32[24]{0:T(128)S(1)} %gather_fusion.3), kind=kOutput, calls=%fused_computation.7.clone.1 | convolution fusion | flops 57016608 | bytes 4718785 | tf_op jit(solution)/shard_map/while/body/eval_jaxpr/sr,sif->rif/dot_general | solution.py:74
  348.0 3.5 gather_fusion
  354.5 6.6 %fusion.66 = f32[6,128,256]{2,0,1:T(8,128)} fusion(f32[24,128,256]{2,1,0:T(8,128)} %fusion.64, f32[6,128,256]{2,0,1:T(8,128)} %get-tuple-element.271, pred[]{:T(512)S(6)} %compare.4, f32[24]{0:T(128)S(1)} %fusion.65, s32[24]{0:T(128)S(1)} %gather_fusion.3), kind=kOutput, calls=%fused_computation.7.clone.1 | convolution fusion | flops 57016608 | bytes 4718785 | tf_op jit(solution)/shard_map/while/body/eval_jaxpr/sr,sif->rif/dot_general | solution.py:74
  363.6 3.5 gather_fusion
  370.1 6.6 %fusion.66 = f32[6,128,256]{2,0,1:T(8,128)} fusion(f32[24,128,256]{2,1,0:T(8,128)} %fusion.64, f32[6,128,256]{2,0,1:T(8,128)} %get-tuple-element.271, pred[]{:T(512)S(6)} %compare.4, f32[24]{0:T(128)S(1)} %fusion.65, s32[24]{0:T(128)S(1)} %gather_fusion.3), kind=kOutput, calls=%fused_computation.7.clone.1 | convolution fusion | flops 57016608 | bytes 4718785 | tf_op jit(solution)/shard_map/while/body/eval_jaxpr/sr,sif->rif/dot_general | solution.py:74
  379.2 3.5 gather_fusion
  385.7 6.6 %fusion.66 = f32[6,128,256]{2,0,1:T(8,128)} fusion(f32[24,128,256]{2,1,0:T(8,128)} %fusion.64, f32[6,128,256]{2,0,1:T(8,128)} %get-tuple-element.271, pred[]{:T(512)S(6)} %compare.4, f32[24]{0:T(128)S(1)} %fusion.65, s32[24]{0:T(128)S(1)} %gather_fusion.3), kind=kOutput, calls=%fused_computation.7.clone.1 | convolution fusion | flops 57016608 | bytes 4718785 | tf_op jit(solution)/shard_map/while/body/eval_jaxpr/sr,sif->rif/dot_general | solution.py:74
  394.8 3.5 gather_fusion
  401.4 6.6 %fusion.66 = f32[6,128,256]{2,0,1:T(8,128)} fusion(f32[24,128,256]{2,1,0:T(8,128)} %fusion.64, f32[6,128,256]{2,0,1:T(8,128)} %get-tuple-element.271, pred[]{:T(512)S(6)} %compare.4, f32[24]{0:T(128)S(1)} %fusion.65, s32[24]{0:T(128)S(1)} %gather_fusion.3), kind=kOutput, calls=%fused_computation.7.clone.1 | convolution fusion | flops 57016608 | bytes 4718785 | tf_op jit(solution)/shard_map/while/body/eval_jaxpr/sr,sif->rif/dot_general | solution.py:74
  410.5 3.5 gather_fusion
  413.9 2.3 fusion.64
  417.0 6.6 %fusion.66 = f32[6,128,256]{2,0,1:T(8,128)} fusion(f32[24,128,256]{2,1,0:T(8,128)} %fusion.64, f32[6,128,256]{2,0,1:T(8,128)} %get-tuple-element.271, pred[]{:T(512)S(6)} %compare.4, f32[24]{0:T(128)S(1)} %fusion.65, s32[24]{0:T(128)S(1)} %gather_fusion.3), kind=kOutput, calls=%fused_computation.7.clone.1 | convolution fusion | flops 57016608 | bytes 4718785 | tf_op jit(solution)/shard_map/while/body/eval_jaxpr/sr,sif->rif/dot_general | solution.py:74
  426.1 3.5 gather_fusion
  432.6 6.6 %fusion.66 = f32[6,128,256]{2,0,1:T(8,128)} fusion(f32[24,128,256]{2,1,0:T(8,128)} %fusion.64, f32[6,128,256]{2,0,1:T(8,128)} %get-tuple-element.271, pred[]{:T(512)S(6)} %compare.4, f32[24]{0:T(128)S(1)} %fusion.65, s32[24]{0:T(128)S(1)} %gather_fusion.3), kind=kOutput, calls=%fused_computation.7.clone.1 | convolution fusion | flops 57016608 | bytes 4718785 | tf_op jit(solution)/shard_map/while/body/eval_jaxpr/sr,sif->rif/dot_general | solution.py:74
  441.7 3.5 gather_fusion
  448.2 6.6 %fusion.66 = f32[6,128,256]{2,0,1:T(8,128)} fusion(f32[24,128,256]{2,1,0:T(8,128)} %fusion.64, f32[6,128,256]{2,0,1:T(8,128)} %get-tuple-element.271, pred[]{:T(512)S(6)} %compare.4, f32[24]{0:T(128)S(1)} %fusion.65, s32[24]{0:T(128)S(1)} %gather_fusion.3), kind=kOutput, calls=%fused_computation.7.clone.1 | convolution fusion | flops 57016608 | bytes 4718785 | tf_op jit(solution)/shard_map/while/body/eval_jaxpr/sr,sif->rif/dot_general | solution.py:74
  460.3 5.0 %fusion.23 = f32[768,2048]{1,0:T(8,128)} fusion(bf16[256,2048]{1,0:T(8,128)(2,1)} %all-gather.4.cloned.1.call-done, f32[768,256]{0,1:T(8,128)S(1)} %get-tuple-element.208, f32[256]{0:T(256)S(1)} %copy-done.5, f32[768]{0:T(1024)S(1)} %add_rsqrt_fusion), kind=kOutput, calls=%fused_computation.41 | convolution fusion | flops 805896192 | bytes 8130560 | tf_op jit(solution)/shard_map/dot_general | solution.py:84
  465.3 5.8 %fusion.22 = bf16[768,256]{0,1:T(8,128)(2,1)S(1)} fusion(f32[768,256]{0,1:T(8,128)S(1)} %get-tuple-element.208, bf16[256,2048]{1,0:T(8,128)(2,1)} %all-gather.8.cloned.1.call-done, f32[768,2048]{1,0:T(8,128)} %fusion.23, bf16[256,2048]{1,0:T(8,128)(2,1)} %all-gather.6.cloned.1.call-done, f32[256]{0:T(256)S(1)} %copy-done.5, f32[768]{0:T(1024)S(1)} %add_rsqrt_fusion), kind=kOutput, calls=%fused_computation.34 | convolution fusion | flops 1621032960 | bytes 9572352 | tf_op jit(solution)/shard_map/dot_general | solution.py:95
  (195 shorter events, 77.2 us)
Async XLA Ops:
  6.5 451.6 %copy-start = (bf16[1024,256]{1,0:T(8,128)(2,1)S(1)}, bf16[1024,256]{1,0:T(8,128)(2,1)}, u32[]{:S(2)}) copy-start(bf16[1024,256]{1,0:T(8,128)(2,1)} %param.23) | copy-start | bytes 1572868
  11.7 12.3 %copy-start.4 = (s32[192,1]{0,1:T(1,128)S(1)}, s32[192,1]{0,1:T(1,128)}, u32[]{:S(2)}) copy-start(s32[192,1]{0,1:T(1,128)} %param.18) | copy-start | bytes 2308
  11.7 14.0 %copy-start.3 = (s32[192,128]{1,0:T(8,128)S(1)}, s32[192,128]{1,0:T(8,128)}, u32[]{:S(2)}) copy-start(s32[192,128]{1,0:T(8,128)} %param.17) | copy-start | bytes 294916
  11.7 193.5 %all-to-all-start = ((bf16[16,1024,256]{2,1,0:T(8,128)(2,1)}), bf16[16,1024,256]{2,1,0:T(8,128)(2,1)}, u32[]{:S(2)}, u32[]{:S(2)}) async-start(bf16[16,1024,256]{2,1,0:T(8,128)(2,1)} %stack.2), calls=%async_computation | async-start | bytes 16777216 | tf_op jit(solution)/shard_map/all_to_all | solution.py:58
  21.8 438.5 %all-gather.4.cloned.1.call-start = ((), (), s32[]{:S(2)}) async-start(), calls=%async_computation.1 | async-start | bytes 1114112 | tf_op jit(solution)/shard_map/all_gather | solution.py:86
  22.5 442.8 %all-gather.6.cloned.1.call-start = ((), (), s32[]{:S(2)}) async-start(), calls=%async_computation.2 | async-start | bytes 1114112 | tf_op jit(solution)/shard_map/all_gather | solution.py:91
  23.2 442.0 %all-gather.8.cloned.1.call-start = ((), (), s32[]{:S(2)}) async-start(), calls=%async_computation.3 | async-start | bytes 1114112 | tf_op jit(solution)/shard_map/all_gather | solution.py:97
  25.6 179.5 %copy-start.1 = (s32[192]{0:T(256)S(1)}, s32[192]{0:T(256)}, u32[]{:S(2)}) copy-start(s32[192]{0:T(256)} %param.19) | copy-start | bytes 2308
  25.6 179.5 %copy-start.2 = (s32[192]{0:T(256)S(1)}, s32[192]{0:T(256)}, u32[]{:S(2)}) copy-start(s32[192]{0:T(256)} %param.20) | copy-start | bytes 2308
  205.2 253.0 %copy-start.6 = (f32[256]{0:T(256)S(1)}, f32[256]{0:T(256)}, u32[]{:S(2)}) copy-start(f32[256]{0:T(256)} %param.21) | copy-start | bytes 3076
  454.8 5.4 %copy-start.5 = (f32[256]{0:T(256)S(1)}, f32[256]{0:T(256)}, u32[]{:S(2)}) copy-start(f32[256]{0:T(256)} %param.24) | copy-start | bytes 3076
Sparse Core Ops, SparseCore 0:
  24.3 58.7 all-gather.3
  84.8 67.4 all-gather.5
  154.0 68.4 all-gather.7
